TPU v7x, 32 devices: a whole 2x2x4 slice. The times are simulated.
32 devices in a mesh: groups: 2 (over y), expert: 4 (over z), tensor: 4 (over x, core), sub: 1.
Axes of the slice: x: 2, y: 2, z: 4, core: 2. Of those that a mesh axis runs over, the one named last changes fastest.
Arguments:
- hidden_rows: bfloat16 [4, 320, 4096], P(None, ('groups', 'expert', 'tensor')), parts along dimension 1, may hold values from -6 to 6
- expert_ids: int32 [4, 320, 8], P(None, ('groups', 'expert', 'tensor')), parts along dimension 1, may hold values from 0 to 15, all different within a row; in each aligned block of 10 rows (0 to 9, 10 to 19, ..., all dimensions but the last counted through in order) at most 5 rows name the same one
- accepted: int32 [4, 64], P(None, ('groups', 'expert', 'tensor')), parts along dimension 1, may hold values from 0 to 4
- norm_gain: float32 [4096], replicated, may hold values from 0.5 to 1.5
- router: bfloat16 [4096, 16], replicated, may hold values from -0.0625 to 0.0625
- gate_weight: bfloat16 [16, 4096, 768], P(('expert', 'tensor'), None, 'sub'), may hold values from -0.09375 to 0.09375
- up_weight: bfloat16 [16, 4096, 768], P(('expert', 'tensor'), None, 'sub'), may hold values from -0.09375 to 0.09375
- down_weight: bfloat16 [16, 768, 4096], P(('expert', 'tensor'), 'sub'), may hold values from -0.21875 to 0.21875
- draft_gain: float32 [4096], replicated, may hold values from 0.5 to 1.5
- draft_gate: bfloat16 [4096, 6144], P(None, ('expert', 'tensor')), may hold values from -0.09375 to 0.09375
- draft_up: bfloat16 [4096, 6144], P(None, ('expert', 'tensor')), may hold values from -0.09375 to 0.09375
- draft_down: bfloat16 [6144, 4096], P(('expert', 'tensor')), may hold values from -0.078125 to 0.078125
- final_gain: float32 [4096], replicated, may hold values from 0.5 to 1.5
Outputs:
- verified: bfloat16 [4, 320, 4096], P(None, ('groups', 'expert', 'tensor')), parts along dimension 1
- draft_out: bfloat16 [4, 64, 4096], P(None, ('groups', 'expert', 'tensor')), parts along dimension 1
There are 2 independent parts, one for each index of `groups`. A program takes and returns all parts, laid end to end along the dimension named above; an argument that names none is the same for every part. Nothing has to cross between parts.
Inputs may be any that keep to these rules, and one draw needn't show every extreme that they name: `expert_ids`: the 8 ids of a row differ. In each aligned block of 10 rows no expert is named by more than 5 rows, and in some block one expert is named by exactly 5 rows.
All inputs are finite; a program needn't handle non-finite values.
Results may differ from a plain program's by a relative error of at most 0.0068.
Values may be sent and summed in bfloat16 or wider, within the bound.
A program may use at most 128 MiB of HBM per device.

v0:
```python
import jax
import jax.numpy as jnp
from jax import lax
from jax.sharding import PartitionSpec as P

EPSILON = 1e-06
RING = ("expert", "tensor")


def rms_scale(values, weights):
    values = values.astype(jnp.float32)
    mean_square = jnp.mean(values * values, axis=-1, keepdims=True)
    return values * lax.rsqrt(mean_square + EPSILON) * weights


def local(
    hidden_rows,
    expert_ids,
    accepted,
    norm_gain,
    router,
    gate_weight,
    up_weight,
    down_weight,
    draft_gain,
    draft_gate,
    draft_up,
    draft_down,
    final_gain,
):
    rounds_total, rows_here, width = hidden_rows.shape
    expert_count = router.shape[1]
    requests_here = accepted.shape[1]
    draft_rows = rows_here // requests_here
    total = rounds_total * rows_here
    my_expert = lax.axis_index(RING)
    rows = hidden_rows.reshape(total, width).astype(jnp.float32)
    normed = rms_scale(rows, norm_gain).astype(jnp.bfloat16)
    logits = jnp.dot(normed, router, preferred_element_type=jnp.float32)
    ids = expert_ids.reshape(total, -1)
    named = jnp.any(ids[:, :, None] == jnp.arange(expert_count, dtype=jnp.int32), axis=1)
    weights = jnp.where(named, jnp.exp(logits), 0.0)
    table = weights / jnp.sum(weights, axis=1, keepdims=True)
    everyone = lax.all_gather(normed, RING, axis=0, tiled=True)
    table = lax.all_gather(table, RING, axis=0, tiled=True)
    share = jnp.sum(
        jnp.where(jnp.arange(expert_count) == my_expert, table, 0.0), axis=1, keepdims=True
    )
    gate_values = jnp.dot(everyone, gate_weight[0], preferred_element_type=jnp.float32)
    up_values = jnp.dot(everyone, up_weight[0], preferred_element_type=jnp.float32)
    active = (jax.nn.silu(gate_values) * up_values).astype(jnp.bfloat16)
    part = jnp.dot(active, down_weight[0], preferred_element_type=jnp.float32)
    part = (share * part).astype(jnp.bfloat16)
    mixed = lax.psum_scatter(part, RING, scatter_dimension=0, tiled=True)
    mixed = lax.psum(mixed, "sub").astype(jnp.float32)
    verified = (rows + mixed).astype(jnp.bfloat16)
    by_request = verified.reshape(rounds_total, requests_here, draft_rows, width)
    pick = jnp.arange(draft_rows, dtype=jnp.int32) == accepted[:, :, None]
    features = jnp.sum(jnp.where(pick[..., None], by_request.astype(jnp.float32), 0.0), axis=2)
    features = features.reshape(rounds_total * requests_here, width)
    draft_input = rms_scale(features, draft_gain).astype(jnp.bfloat16)
    pieces = lax.all_gather(draft_input, RING, axis=0, tiled=True)
    gate_part = jnp.dot(pieces, draft_gate, preferred_element_type=jnp.float32)
    up_part = jnp.dot(pieces, draft_up, preferred_element_type=jnp.float32)
    units = (jax.nn.silu(gate_part) * up_part).astype(jnp.bfloat16)
    summed = lax.psum_scatter(
        jnp.dot(units, draft_down, preferred_element_type=jnp.float32).astype(jnp.bfloat16),
        RING,
        scatter_dimension=0,
        tiled=True,
    ).astype(jnp.float32)
    draft_out = rms_scale(features + summed, final_gain).astype(jnp.bfloat16)
    return (
        verified.reshape(hidden_rows.shape),
        draft_out.reshape(rounds_total, requests_here, width),
    )


def solution(mesh):
    placed = (
        P(None, ("groups", "expert", "tensor"), None),
        P(None, ("groups", "expert", "tensor"), None),
        P(None, ("groups", "expert", "tensor")),
        P(),
        P(),
        P(("expert", "tensor"), None, "sub"),
        P(("expert", "tensor"), None, "sub"),
        P(("expert", "tensor"), "sub", None),
        P(),
        P(None, ("expert", "tensor")),
        P(None, ("expert", "tensor")),
        P(("expert", "tensor"), None),
        P(),
    )
    return jax.shard_map(
        local,
        mesh=mesh,
        in_specs=placed,
        out_specs=(
            P(None, ("groups", "expert", "tensor"), None),
            P(None, ("groups", "expert", "tensor"), None),
        ),
        check_vma=False,
    )
```

profile of v0, /device:TPU:0, one launch (start us, length us, event | category | flops | bytes accessed | tf_op | source)
XLA Modules:
  0.0 299.9 jit_solution(18209610796333644949)
XLA Ops:
  7.2 2.3 copy.37
  9.5 1.2 multiply_reduce_fusion
  10.8 2.2 reshape.74
  13.0 0.1 copy.43
  13.1 1.9 multiply_convert_fusion.2
  15.2 0.7 copy.38
  16.0 1.2 fusion.21
  17.2 24.0 %all-gather = f32[16,40,16]{1,2,0:T(8,128)S(1)} all-gather(f32[1,40,16]{1,2,0:T(8,128)S(1)} %divide_bitcast_fusion), channel_id=1, replica_groups=mesh['groups'=2,'expert'=4,'tensor'=4,'sub'=1] {'expert','tensor'}, dimensions={0}, use_global_device_ids=true | all-gather | bytes 43520 | tf_op jit(solution)/shard_map/all_gather | solution.py:45
  41.3 0.1 reshape.77
  41.4 0.1 select_reduce_fusion.1
  41.5 32.6 %all-gather.4.cloned.1.call-done = bf16[640,4096]{1,0:T(8,128)(2,1)} async-done(((bf16[40,4096]{1,0:T(8,128)(2,1)}), bf16[640,4096]{1,0:T(8,128)(2,1)}) %all-gather.4.cloned.1.call-update) | async-done | bytes 5242896 | tf_op jit(solution)/shard_map/all_gather | solution.py:44
  74.1 9.8 %fusion.3 = f32[640,768]{1,0:T(8,128)} fusion(bf16[640,4096]{1,0:T(8,128)(2,1)} %all-gather.4.cloned.1.call-done, bf16[1,4096,768]{2,1,0:T(8,128)(2,1)} %param.18), kind=kOutput, calls=%fused_computation.4 | convolution fusion | flops 4026531840 | bytes 13500416 | tf_op jit(solution)/shard_map/dot_general | solution.py:49
  83.9 18.5 %multiply_convert_fusion = bf16[640,4096]{1,0:T(8,128)(2,1)} fusion(bf16[1,768,4096]{2,1,0:T(8,128)(2,1)} %param.20, f32[640]{0:T(1024)S(1)} %select_reduce_fusion.1, f32[640,768]{1,0:T(8,128)} %fusion.3, bf16[640,4096]{1,0:T(8,128)(2,1)} %all-gather.4.cloned.1.call-done, bf16[1,4096,768]{2,1,0:T(8,128)(2,1)} %param.19), kind=kOutput, calls=%fused_computation | convolution fusion | flops 8061255680 | bytes 25037312 | tf_op jit(solution)/shard_map/dot_general | solution.py:52
  102.4 0.6 copy-done.3
  103.0 0.1 copy.41
  103.2 76.3 %reduce-scatter.3.cloned.1.call-done = bf16[40,4096]{1,0:T(8,128)(2,1)} async-done(((bf16[640,4096]{1,0:T(8,128)(2,1)}), bf16[40,4096]{1,0:T(8,128)(2,1)}) %reduce-scatter.3.cloned.1.call-update) | async-done | bytes 327696 | tf_op jit(solution)/shard_map/reduce_scatter | solution.py:54
  179.5 1.2 add_convert_fusion
  180.8 1.1 reshape.75
  181.9 2.4 select_reduce_fusion
  184.2 1.6 reshape.72
  185.9 1.1 multiply_reduce_fusion.2
  187.0 1.6 multiply_convert_fusion.4
  188.7 0.2 reduce-scatter.5.cloned.1.call-start
  188.9 36.9 %all-gather.6.cloned.1.call-done = bf16[128,4096]{1,0:T(8,128)(2,1)} async-done(((bf16[8,4096]{1,0:T(8,128)(2,1)}), bf16[128,4096]{1,0:T(8,128)(2,1)}) %all-gather.6.cloned.1.call-update) | async-done | bytes 1048592 | tf_op jit(solution)/shard_map/all_gather | solution.py:62
  225.8 3.6 %fusion.22 = f32[128,384]{1,0:T(8,128)} fusion(bf16[128,4096]{1,0:T(8,128)(2,1)} %all-gather.6.cloned.1.call-done, bf16[4096,384]{1,0:T(8,128)(2,1)} %param.22), kind=kOutput, calls=%fused_computation.40 | convolution fusion | flops 402653184 | bytes 4390912 | tf_op jit(solution)/shard_map/dot_general | solution.py:63
  229.4 4.6 %convolution_convert_fusion = bf16[128,4096]{1,0:T(8,128)(2,1)} fusion(bf16[384,4096]{1,0:T(8,128)(2,1)S(1)} %copy-done, bf16[128,4096]{1,0:T(8,128)(2,1)} %all-gather.6.cloned.1.call-done, bf16[4096,384]{1,0:T(8,128)(2,1)} %param.23, f32[128,384]{1,0:T(8,128)} %fusion.22), kind=kOutput, calls=%fused_computation.6 | convolution fusion | flops 806125568 | bytes 8585216 | tf_op jit(solution)/shard_map/dot_general | solution.py:67
  234.0 0.9 reshape.71
  234.9 2.0 copy.42
  237.0 53.7 %reduce-scatter.5.cloned.1.call-done = bf16[8,4096]{1,0:T(8,128)(2,1)} async-done(((bf16[128,4096]{1,0:T(8,128)(2,1)}), bf16[8,4096]{1,0:T(8,128)(2,1)}) %reduce-scatter.5.cloned.1.call-update) | async-done | bytes 65552 | tf_op jit(solution)/shard_map/reduce_scatter | solution.py:66
  290.7 1.1 multiply_reduce_fusion.1
  291.7 1.0 multiply_convert_fusion.3
  292.7 0.7 reshape.73
  (25 shorter events, 0.6 us)
Async XLA Ops:
  7.2 222.2 %copy-start = (bf16[384,4096]{1,0:T(8,128)(2,1)S(1)}, bf16[384,4096]{1,0:T(8,128)(2,1)}, u32[]{:S(2)}) copy-start(bf16[384,4096]{1,0:T(8,128)(2,1)} %param.24) | copy-start | bytes 9437188
  7.2 66.9 %all-gather.4.cloned.1.call-start = ((), (), s32[]{:S(2)}) async-start(), calls=%async_computation.2 | async-start | bytes 5570560 | tf_op jit(solution)/shard_map/all_gather | solution.py:44
  15.1 164.4 %reduce-scatter.3.cloned.1.call-start = ((), (), s32[]{:S(2)}) async-start(), calls=%async_computation.3 | async-start | bytes 5570560 | tf_op jit(solution)/shard_map/reduce_scatter | solution.py:54
  102.4 0.7 copy-start.3
  102.4 84.7 %copy-start.2 = (f32[4096]{0:T(1024)S(1)}, f32[4096]{0:T(1024)}, u32[]{:S(2)}) copy-start(f32[4096]{0:T(1024)} %param.21) | copy-start | bytes 49156
  102.4 123.4 %all-gather.6.cloned.1.call-start = ((), (), s32[]{:S(2)}) async-start(), calls=%async_computation.4 | async-start | bytes 1114112 | tf_op jit(solution)/shard_map/all_gather | solution.py:62
  188.7 102.0 %reduce-scatter.5.cloned.1.call-start = ((), (), s32[]{:S(2)}) async-start(), calls=%async_computation.5 | async-start | bytes 1114112 | tf_op jit(solution)/shard_map/reduce_scatter | solution.py:66
  229.4 62.3 %copy-start.1 = (f32[4096]{0:T(1024)S(1)}, f32[4096]{0:T(1024)}, u32[]{:S(2)}) copy-start(f32[4096]{0:T(1024)} %param.25) | copy-start | bytes 49156
Sparse Core Ops, SparseCore 0:
  15.2 58.7 all-gather.3
  102.5 76.9 reduce-scatter.2
  188.8 36.9 all-gather.5
  234.1 56.4 reduce-scatter.4
where the time goes:
time: 301 us; the launch traced here: 300 us
  waiting for transfers between devices  200 us (66%)
  matrix products  37.7 us (13%)
  blocking collectives  24 us (8%)
  between operations  13.8 us (5%)
  local copies, waits for them, and re-layouts  12.8 us (4%)
  other arithmetic  11.7 us (4%)
    reduce_scatter x1, waiting for transfers between devices, local(): mixed = lax.psum_scatter(part, RING, scatter_dimension=0, tiled=True)  76.3 us
    reduce_scatter x1, waiting for transfers between devices, local(): lax.psum_scatter(jnp.dot(units, draft_down, preferred_element_type=jnp.fl...  53.7 us
    all_gather x1, waiting for transfers between devices, local(): pieces = lax.all_gather(draft_input, RING, axis=0, tiled=True)  36.9 us
    all_gather x1, waiting for transfers between devices, local(): everyone = lax.all_gather(normed, RING, axis=0, tiled=True)  32.6 us
    all_gather x1, blocking collectives, local(): table = lax.all_gather(table, RING, axis=0, tiled=True)  24 us
    dot_general x1, matrix products, local(): part = jnp.dot(active, down_weight[0], preferred_element_type=jnp.float32)  18.5 us
    dot_general x1, matrix products, local(): jnp.dot(everyone, gate_weight[0], preferred_element_type=jnp.float32)  9.83 us
  transfers between devices with their start and end apart: 4, of which 4 were waited for; matrix products, arithmetic and copies ran while one was open for 2% of the time, Pallas kernels for 0%

commit v1 on v0

--- a/solution.py
+++ b/solution.py
@@ -5,6 +5,14 @@
 
 EPSILON = 1e-06
 RING = ("expert", "tensor")
+
+
+def manage_the_turns(original, m):
+    return jnp.split(
+        jax.lax.all_gather(jnp.concatenate([original, m], axis=1), RING, axis=0, tiled=True),
+        [original.shape[1]],
+        axis=1,
+    )
 
 
 def rms_scale(values, weights):
@@ -41,8 +49,7 @@
     named = jnp.any(ids[:, :, None] == jnp.arange(expert_count, dtype=jnp.int32), axis=1)
     weights = jnp.where(named, jnp.exp(logits), 0.0)
     table = weights / jnp.sum(weights, axis=1, keepdims=True)
-    everyone = lax.all_gather(normed, RING, axis=0, tiled=True)
-    table = lax.all_gather(table, RING, axis=0, tiled=True)
+    everyone, table = manage_the_turns(normed, table)
     share = jnp.sum(
         jnp.where(jnp.arange(expert_count) == my_expert, table, 0.0), axis=1, keepdims=True
     )

time: 301 us -> 332 us (1.10)
  waiting for transfers between devices: 200 us -> 259 us
  blocking collectives: 24 us -> 0 us
  matrix products: 37.7 us -> 31.8 us
    all_gather x1, waiting for transfers between devices: 32.6 us -> 92.4 us  [manage_the_turns(): jax.lax.all_gather(jnp.concatenate([original, m], axis=1), RING, axis=0,...]
    all_gather x1 -> x0, blocking collectives: 24 us -> none  [local(): table = lax.all_gather(table, RING, axis=0, tiled=True)]
    dot_general x1, matrix products: 18.5 us -> 5.96 us  [local(): part = jnp.dot(active, down_weight[0], preferred_element_type=jnp.float32)]
    dot_general x0 -> x1, matrix products: none -> 7.34 us  [local(): jnp.dot(everyone, up_weight[0], preferred_element_type=jnp.float32)]
  transfers between devices with their start and end apart: 4 -> 4, of which waited for: 4 -> 4; matrix products, arithmetic and copies ran while one was open for 2% -> 1% of each run, Pallas kernels for 0% -> 0%
where the time goes in v1:
time: 332 us
  waiting for transfers between devices  259 us (78%)
  matrix products  31.8 us (10%)
  other arithmetic  13.9 us (4%)
  between operations  13.9 us (4%)
  local copies, waits for them, and re-layouts  12.7 us (4%)
    all_gather x1, waiting for transfers between devices, manage_the_turns(): jax.lax.all_gather(jnp.concatenate([original, m], axis=1), RING, axis=0,...  92.4 us
    reduce_scatter x1, waiting for transfers between devices, local(): mixed = lax.psum_scatter(part, RING, scatter_dimension=0, tiled=True)  75.9 us
    reduce_scatter x1, waiting for transfers between devices, local(): lax.psum_scatter(jnp.dot(units, draft_down, preferred_element_type=jnp.fl...  53.8 us
    all_gather x1, waiting for transfers between devices, local(): pieces = lax.all_gather(draft_input, RING, axis=0, tiled=True)  37.1 us
    dot_general x1, matrix products, local(): jnp.dot(everyone, gate_weight[0], preferred_element_type=jnp.float32)  8.91 us
    dot_general x1, matrix products, local(): jnp.dot(everyone, up_weight[0], preferred_element_type=jnp.float32)  7.34 us
  transfers between devices with their start and end apart: 4, of which 4 were waited for; matrix products, arithmetic and copies ran while one was open for 1% of the time, Pallas kernels for 0%

profile of v1, /device:TPU:0, one launch (start us, length us, event | category | flops | bytes accessed | tf_op | source)
XLA Modules:
  0.0 331.7 jit_solution(17097548730330170784)
XLA Ops:
  7.2 2.3 copy.38
  9.5 1.2 multiply_reduce_fusion
  10.8 2.1 reshape.74
  12.9 0.1 copy.44
  13.0 0.1 rsqrt.31
  13.1 0.7 copy.40
  13.9 2.1 fusion.22
  16.0 1.4 fusion.23
  17.5 2.0 pad_maximum_fusion
  19.6 92.4 %all-gather.3.cloned.1.call-done = f32[640,4112]{1,0:T(8,128)} async-done(((f32[40,4112]{1,0:T(8,128)}), f32[640,4112]{1,0:T(8,128)}) %all-gather.3.cloned.1.call-update) | async-done | bytes 10526736 | tf_op jit(solution)/shard_map/all_gather | solution.py:12
  112.0 8.9 %fusion.2 = f32[640,768]{1,0:T(8,128)S(1)} fusion(f32[640,4112]{1,0:T(8,128)} %all-gather.3.cloned.1.call-done, bf16[1,4096,768]{2,1,0:T(8,128)(2,1)} %param.18), kind=kOutput, calls=%fused_computation.3 | convolution fusion | flops 4026531840 | bytes 13500416 | tf_op jit(solution)/shard_map/dot_general | solution.py:56
  120.9 0.2 fusion.13
  121.1 7.3 %multiply_convert_fusion.1 = bf16[640,768]{1,0:T(8,128)(2,1)S(1)} fusion(f32[640,768]{1,0:T(8,128)S(1)} %fusion.2, bf16[1,4096,768]{2,1,0:T(8,128)(2,1)} %param.19, f32[640,4112]{1,0:T(8,128)S(1)} %copy-done.3), kind=kOutput, calls=%fused_computation.9 | convolution fusion | flops 4029480960 | bytes 14483456 | tf_op jit(solution)/shard_map/dot_general | solution.py:57
  128.5 6.0 %multiply_convert_fusion = bf16[640,4096]{1,0:T(8,128)(2,1)} fusion(bf16[640,768]{1,0:T(8,128)(2,1)S(1)} %multiply_convert_fusion.1, bf16[1,768,4096]{2,1,0:T(8,128)(2,1)S(1)} %bitcast.21, f32[640]{0:T(1024)S(1)} %fusion.13), kind=kOutput, calls=%fused_computation | convolution fusion | flops 4031774720 | bytes 12519936 | tf_op jit(solution)/shard_map/dot_general | solution.py:59
  134.5 0.6 copy-done.4
  135.1 0.1 copy.42
  135.3 75.9 %reduce-scatter.3.cloned.1.call-done = bf16[40,4096]{1,0:T(8,128)(2,1)} async-done(((bf16[640,4096]{1,0:T(8,128)(2,1)}), bf16[40,4096]{1,0:T(8,128)(2,1)}) %reduce-scatter.3.cloned.1.call-update) | async-done | bytes 327696 | tf_op jit(solution)/shard_map/reduce_scatter | solution.py:61
  211.2 1.2 add_convert_fusion
  212.5 1.1 reshape.75
  213.6 2.4 select_reduce_fusion
  215.9 1.6 reshape.72
  217.6 1.1 multiply_reduce_fusion.2
  218.7 1.6 multiply_convert_fusion.4
  220.4 37.1 %all-gather.5.cloned.1.call-done = bf16[128,4096]{1,0:T(8,128)(2,1)} async-done(((bf16[8,4096]{1,0:T(8,128)(2,1)}), bf16[128,4096]{1,0:T(8,128)(2,1)}) %all-gather.5.cloned.1.call-update) | async-done | bytes 1048592 | tf_op jit(solution)/shard_map/all_gather | solution.py:69
  257.5 3.6 %fusion.24 = f32[128,384]{1,0:T(8,128)} fusion(bf16[128,4096]{1,0:T(8,128)(2,1)} %all-gather.5.cloned.1.call-done, bf16[4096,384]{1,0:T(8,128)(2,1)} %param.22), kind=kOutput, calls=%fused_computation.43 | convolution fusion | flops 402653184 | bytes 4390912 | tf_op jit(solution)/shard_map/dot_general | solution.py:70
  261.1 4.6 %convolution_convert_fusion = bf16[128,4096]{1,0:T(8,128)(2,1)} fusion(bf16[384,4096]{1,0:T(8,128)(2,1)S(1)} %copy-done, bf16[128,4096]{1,0:T(8,128)(2,1)} %all-gather.5.cloned.1.call-done, bf16[4096,384]{1,0:T(8,128)(2,1)} %param.23, f32[128,384]{1,0:T(8,128)} %fusion.24), kind=kOutput, calls=%fused_computation.8 | convolution fusion | flops 806125568 | bytes 8585216 | tf_op jit(solution)/shard_map/dot_general | solution.py:74
  265.7 0.9 reshape.71
  266.6 2.0 copy.43
  268.7 53.8 %reduce-scatter.5.cloned.1.call-done = bf16[8,4096]{1,0:T(8,128)(2,1)} async-done(((bf16[128,4096]{1,0:T(8,128)(2,1)}), bf16[8,4096]{1,0:T(8,128)(2,1)}) %reduce-scatter.5.cloned.1.call-update) | async-done | bytes 65552 | tf_op jit(solution)/shard_map/reduce_scatter | solution.py:73
  322.4 1.1 multiply_reduce_fusion.1
  323.5 1.0 multiply_convert_fusion.3
  324.5 0.7 reshape.73
  (32 shorter events, 0.6 us)
Async XLA Ops:
  7.2 254.0 %copy-start = (bf16[384,4096]{1,0:T(8,128)(2,1)S(1)}, bf16[384,4096]{1,0:T(8,128)(2,1)}, u32[]{:S(2)}) copy-start(bf16[384,4096]{1,0:T(8,128)(2,1)} %param.24) | copy-start | bytes 9437188
  7.2 104.8 %all-gather.3.cloned.1.call-start = ((), (), s32[]{:S(2)}) async-start(), calls=%async_computation.2 | async-start | bytes 11489280 | tf_op jit(solution)/shard_map/all_gather | solution.py:12
  19.5 191.7 %reduce-scatter.3.cloned.1.call-start = ((), (), s32[]{:S(2)}) async-start(), calls=%async_computation.3 | async-start | bytes 5570560 | tf_op jit(solution)/shard_map/reduce_scatter | solution.py:61
  112.0 8.9 %copy-start.3 = (f32[640,4112]{1,0:T(8,128)S(1)}, f32[640,4112]{1,0:T(8,128)}, u32[]{:S(2)}) copy-start(f32[640,4112]{1,0:T(8,128)} %all-gather.3.cloned.1.call-done) | copy-start | bytes 31580164
  112.0 16.5 %slice-start = ((s8[6291456]{0:T(1024)(128)(4,1)}), s8[4194304]{0:T(1024)(128)(4,1)S(1)}, s32[]{:S(2)}) async-start(s8[6291456]{0:T(1024)(128)(4,1)} %bitcast.20), calls=%async_computation.6 | async-start | bytes 8388608
  121.1 7.4 %slice-start.1 = ((s8[6291456]{0:T(1024)(128)(4,1)}), s8[2097152]{0:T(1024)(128)(4,1)S(1)}, s32[]{:S(2)}) async-start(s8[6291456]{0:T(1024)(128)(4,1)} %bitcast.20), calls=%async_computation.7 | async-start | bytes 4194304
  134.4 0.7 copy-start.4
  134.4 84.3 %copy-start.2 = (f32[4096]{0:T(1024)S(1)}, f32[4096]{0:T(1024)}, u32[]{:S(2)}) copy-start(f32[4096]{0:T(1024)} %param.21) | copy-start | bytes 49156
  134.5 123.0 %all-gather.5.cloned.1.call-start = ((), (), s32[]{:S(2)}) async-start(), calls=%async_computation.4 | async-start | bytes 1114112 | tf_op jit(solution)/shard_map/all_gather | solution.py:69
  220.4 102.1 %reduce-scatter.5.cloned.1.call-start = ((), (), s32[]{:S(2)}) async-start(), calls=%async_computation.5 | async-start | bytes 1114112 | tf_op jit(solution)/shard_map/reduce_scatter | solution.py:73
  261.1 62.4 %copy-start.1 = (f32[4096]{0:T(1024)S(1)}, f32[4096]{0:T(1024)}, u32[]{:S(2)}) copy-start(f32[4096]{0:T(1024)} %param.25) | copy-start | bytes 49156
Sparse Core Ops, SparseCore 0:
  19.6 92.2 all-gather.2
  134.6 76.6 reduce-scatter.2
  220.5 36.9 all-gather.4
  265.8 56.5 reduce-scatter.4
